TPU v7x, 256 devices: a whole 4x4x8 slice. The times are simulated.
256 devices in a mesh: leaf: 32 (over z, y), head: 8 (over x, core).
Axes of the slice: x: 4, y: 4, z: 8, core: 2. Of those that a mesh axis runs over, the one named last changes fastest.
Arguments:
- query_in: bfloat16 [4096, 8192], P('leaf', 'head'), may hold values from -12 to 12
- key_in: bfloat16 [4096, 1024], P(('leaf', 'head')), may hold values from -12 to 12
- value_in: bfloat16 [4096, 1024], P(('leaf', 'head')), may hold values from -6 to 6
- out_grad: bfloat16 [4096, 8192], P('leaf', 'head'), may hold values from -6 to 6
- ancestry: int32 [32, 8], replicated, may hold values from -1 to 31, as said below
- node_len: int32 [32], replicated, may hold values from 64 to 128, as said below
Outputs:
- attended: bfloat16 [4096, 8192], P('leaf', 'head')
- query_grad: float32 [4096, 8192], P('leaf', 'head')
- key_grad: float32 [4096, 1024], P(('leaf', 'head'))
- value_grad: float32 [4096, 1024], P(('leaf', 'head'))
Inputs may be any that keep to these rules, and one draw needn't show every extreme that they name: `ancestry`: row g lists the ancestors of node g from the root, node 0, at column 0 down to node g itself at column depth(g), then -1; every ancestor of a node comes before it; nodes 0 to 3 form a chain. `node_len`: the root's length is 128, the last node's 128 // 2.
All inputs are finite; a program needn't handle non-finite values.
Results may differ from a plain program's by a relative error of at most 0.019.
Values may be sent and summed in bfloat16 or wider, within the bound.
No kernel may reach another device: no remote copies, remote signals or barrier semaphores. Data moves between devices by JAX's collectives and lax.ppermute only.
A program may use at most 64 MiB of HBM per device.

v0:
```python
import math
import jax
import jax.numpy as jnp
from jax import lax
from jax.sharding import PartitionSpec as P

QH = 64
KVH = 8
HD = 128
BLK = 128
start_level = -1e30
tile_rows = 256


def over_tiles(length, update, carry):
    tile_width = math.gcd(length, tile_rows)
    return lax.fori_loop(
        0,
        length // tile_width,
        lambda number, state: update(state, number * tile_width, tile_width),
        carry,
    )


def token_tags(length_table, first, amount):
    position = first + jnp.arange(amount, dtype=jnp.int32)
    lengths = lax.dynamic_slice_in_dim(length_table, first, amount, 0)
    return (jnp.where(position % BLK < lengths, position // BLK, -2), position)


def visible(ancestor_rows, query_position, key_tag, key_position):
    member = jnp.any(ancestor_rows[:, :, None] == key_tag[None, None, :], axis=1)
    own_node = query_position // BLK
    return member & (
        (key_tag[None, :] != own_node[:, None]) | (key_position[None, :] <= query_position[:, None])
    )


def logits_of(query_group, key_tile, allowed):
    key_count = key_tile.shape[0]
    key_rows = key_tile.reshape(key_count, query_group.shape[1], HD)
    raw = jnp.einsum(
        "tkgd,skd->kgts", query_group, key_rows, preferred_element_type=jnp.float32
    ) * HD ** (-0.5)
    return jnp.where(allowed[None, None], raw, -jnp.inf)


def forward_tile(state, query_group, key_tile, value_tile, allowed):
    row_top, total, accum = state
    logits = logits_of(query_group, key_tile, allowed)
    new_top = jnp.maximum(row_top, jnp.max(logits, axis=-1))
    factor = jnp.exp(row_top - new_top)
    expo = jnp.exp(logits - new_top[..., None])
    total = total * factor + jnp.sum(expo, axis=-1)
    value_rows = value_tile.reshape(value_tile.shape[0], query_group.shape[1], HD)
    accum = accum * factor[..., None] + jnp.einsum(
        "kgts,skd->kgtd", expo.astype(jnp.bfloat16), value_rows, preferred_element_type=jnp.float32
    )
    return (new_top, total, accum)


def gradient_tile(query_group, grad_group, lse, delta, key_tile, value_tile, allowed):
    logits = logits_of(query_group, key_tile, allowed)
    weights = jnp.exp(logits - lse[..., None])
    value_rows = value_tile.reshape(value_tile.shape[0], query_group.shape[1], HD)
    dprob = jnp.einsum("tkgd,skd->kgts", grad_group, value_rows, preferred_element_type=jnp.float32)
    dlogit = (weights * (dprob - delta[..., None])).astype(jnp.bfloat16)
    return (weights.astype(jnp.bfloat16), dlogit)


def per_device(query_in, key_in, value_in, out_grad, ancestry, node_len):
    key_local, value_local = (
        lax.all_to_all(key_in, "head", split_axis=1, concat_axis=0, tiled=True),
        lax.all_to_all(value_in, "head", split_axis=1, concat_axis=0, tiled=True),
    )
    rows = query_in.shape[0]
    key_heads = key_local.shape[1] // HD
    group = QH // KVH
    leaf_base = lax.axis_index("leaf") * rows
    length_table = jnp.repeat(node_len, BLK)
    ancestor_table = jnp.repeat(ancestry, BLK, axis=0)
    all_rows = length_table.shape[0]
    query_position = leaf_base + jnp.arange(rows, dtype=jnp.int32)
    query_ancestors = lax.dynamic_slice_in_dim(ancestor_table, leaf_base, rows, 0)
    query_group = query_in.reshape(rows, key_heads, group, HD)
    grad_group = out_grad.reshape(rows, key_heads, group, HD)
    initial = (
        jnp.full((key_heads, group, rows), start_level, jnp.float32),
        jnp.zeros((key_heads, group, rows), jnp.float32),
        jnp.zeros((key_heads, group, rows, HD), jnp.float32),
    )
    key_piece = lax.all_gather(key_local, "leaf", axis=0, tiled=True)
    value_piece = lax.all_gather(value_local, "leaf", axis=0, tiled=True)

    def update(inner, offset, tile_width):
        key_tile = lax.dynamic_slice_in_dim(key_piece, offset, tile_width, 0)
        value_tile = lax.dynamic_slice_in_dim(value_piece, offset, tile_width, 0)
        key_tag, key_position = token_tags(length_table, offset, tile_width)
        allowed = visible(query_ancestors, query_position, key_tag, key_position)
        return forward_tile(inner, query_group, key_tile, value_tile, allowed)

    row_top, total, accum = over_tiles(key_piece.shape[0], update, initial)
    key_all, value_all = (
        lax.all_gather(key_local, "leaf", axis=0, tiled=True),
        lax.all_gather(value_local, "leaf", axis=0, tiled=True),
    )
    output = (accum / total[..., None]).astype(jnp.bfloat16)
    log_total = row_top + jnp.log(total)
    delta = jnp.sum(
        grad_group.transpose(1, 2, 0, 3).astype(jnp.float32) * output.astype(jnp.float32), axis=-1
    )
    attended = output.transpose(2, 0, 1, 3).reshape(rows, key_heads * group * HD)
    query_zero = jnp.zeros((rows, key_heads, group, HD), jnp.float32)

    def update_both(state, offset, tile_width):
        query_acc, buffer = state
        key_tile = lax.dynamic_slice_in_dim(key_all, offset, tile_width, 0)
        value_tile = lax.dynamic_slice_in_dim(value_all, offset, tile_width, 0)
        key_tag, key_position = token_tags(length_table, offset, tile_width)
        allowed = visible(query_ancestors, query_position, key_tag, key_position)
        probs, dlogit = gradient_tile(
            query_group, grad_group, log_total, delta, key_tile, value_tile, allowed
        )
        key_rows = key_tile.reshape(tile_width, key_heads, HD)
        query_acc = query_acc + jnp.einsum(
            "kgts,skd->tkgd", dlogit, key_rows, preferred_element_type=jnp.float32
        )
        key_term = jnp.einsum(
            "kgts,tkgd->skd", dlogit, query_group, preferred_element_type=jnp.float32
        )
        value_term = jnp.einsum(
            "kgts,tkgd->skd", probs, grad_group, preferred_element_type=jnp.float32
        )
        both_terms = jnp.concatenate(
            [
                key_term.reshape(tile_width, key_heads * HD),
                value_term.reshape(tile_width, key_heads * HD),
            ],
            axis=1,
        )
        buffer = lax.dynamic_update_slice_in_dim(buffer, both_terms, offset, 0)
        return (query_acc, buffer)

    buffer_zero = jnp.zeros((all_rows, 2 * key_heads * HD), jnp.float32)
    query_sum, buffer = over_tiles(all_rows, update_both, (query_zero, buffer_zero))
    summed = lax.psum_scatter(
        buffer.astype(jnp.bfloat16), "leaf", scatter_dimension=0, tiled=True
    ).astype(jnp.float32)
    key_sum = summed[:, : key_heads * HD]
    value_grad = summed[:, key_heads * HD :]
    scale = HD ** (-0.5)
    query_grad = (query_sum * scale).reshape(rows, key_heads * group * HD)
    key_grad = key_sum * scale
    key_grad, value_grad = (
        lax.all_to_all(
            key_grad.astype(jnp.bfloat16), "head", split_axis=0, concat_axis=1, tiled=True
        ).astype(key_grad.dtype),
        lax.all_to_all(
            value_grad.astype(jnp.bfloat16), "head", split_axis=0, concat_axis=1, tiled=True
        ).astype(value_grad.dtype),
    )
    return (attended, query_grad, key_grad, value_grad)


def solution(mesh):
    return jax.shard_map(
        per_device,
        mesh=mesh,
        in_specs=(
            P("leaf", "head"),
            P(("leaf", "head"), None),
            P(("leaf", "head"), None),
            P("leaf", "head"),
            P(),
            P(),
        ),
        out_specs=(
            P("leaf", "head"),
            P("leaf", "head"),
            P(("leaf", "head"), None),
            P(("leaf", "head"), None),
        ),
        check_vma=False,
    )
```

profile of v0, /device:TPU:1, one launch (start us, length us, event | category | flops | bytes accessed | tf_op | source)
XLA Modules:
  0.0 555.6 jit_solution(12811123765744551282)
XLA Ops:
  7.9 11.0 %all_to_all.64 = bf16[16,8,128]{2,0,1:T(8,128)(2,1)} all-to-all(bf16[16,8,128]{2,0,1:T(8,128)(2,1)S(1)} %copy_bitcast_fusion.3), channel_id=1, replica_groups=mesh['leaf'=32,'head'=8] {'head'}, dimensions={1} | all-to-all | bytes 65536 | tf_op jit(solution)/shard_map/all_to_all | solution.py:73
  19.7 8.5 %all_to_all.65 = bf16[16,8,128]{2,0,1:T(8,128)(2,1)} all-to-all(bf16[16,8,128]{2,0,1:T(8,128)(2,1)S(1)} %copy_bitcast_fusion.2), channel_id=1, replica_groups=mesh['leaf'=32,'head'=8] {'head'}, dimensions={1} | all-to-all | bytes 65536 | tf_op jit(solution)/shard_map/all_to_all | solution.py:74
  31.8 59.2 %all-gather.3.cloned.1.call-done = bf16[4096,128]{1,0:T(8,128)(2,1)} async-done(((bf16[128,128]{1,0:T(8,128)(2,1)}), bf16[4096,128]{1,0:T(8,128)(2,1)}) %all-gather.3.cloned.1.call-update) | async-done | bytes 1048592 | tf_op jit(solution)/shard_map/all_gather | solution.py:92
  91.0 76.5 %all-gather.5.cloned.1.call-done = bf16[4096,128]{1,0:T(8,128)(2,1)} async-done(((bf16[128,128]{1,0:T(8,128)(2,1)}), bf16[4096,128]{1,0:T(8,128)(2,1)}) %all-gather.5.cloned.1.call-update) | async-done | bytes 1048592 | tf_op jit(solution)/shard_map/all_gather | solution.py:93
  167.5 56.2 %while.44 = (s32[]{:T(128)}, f32[1,8,128]{2,1,0:T(8,128)S(1)}, f32[1,8,128]{2,1,0:T(8,128)S(1)}, f32[1,8,128,128]{3,2,1,0:T(8,128)S(1)}, s32[128,8]{1,0:T(8,128)...) while((s32[]{:T(128)}, f32[1,8,128]{2,1,0:T(8,128)S(1)}, ...), condition=%wide.region_4.5_spmd.clone.clone.clone, body=%wide.region_0.4_spmd.clone.clone.clone.sunk | while | flops 137082496 | bytes 4862171 | solution.py:17
  169.6 1.4 fusion.87
  173.1 1.4 fusion.87
  176.6 1.4 fusion.87
  180.1 1.4 fusion.87
  183.6 1.4 fusion.87
  187.1 1.4 fusion.87
  190.7 1.4 fusion.87
  194.2 1.4 fusion.87
  197.7 1.4 fusion.87
  201.2 1.4 fusion.87
  204.7 1.4 fusion.87
  208.2 1.4 fusion.87
  211.7 1.4 fusion.87
  215.2 1.4 fusion.87
  218.8 1.4 fusion.87
  222.3 1.4 fusion.87
  224.8 81.0 %while.45 = (s32[]{:T(128)}, f32[128,1,8,128]{0,3,2,1:T(8,128)S(1)}, bf16[4096,256]{1,0:T(8,128)(2,1)S(1)}, bf16[4096,128]{1,0:T(8,128)(2,1)}, s32[128,8]{1,0:T(...) while((s32[]{:T(128)}, ...), condition=%wide.region_8.9_spmd.clone.clone.clone, body=%wide.region_6.8_spmd.clone.clone.clone.sunk | while | flops 338534016 | bytes 8147185 | solution.py:17
  225.6 1.2 fusion.99
  230.7 1.2 fusion.99
  235.7 1.2 fusion.99
  238.7 1.2 fusion.101
  240.8 1.2 fusion.99
  245.8 1.2 fusion.99
  250.9 1.2 fusion.99
  253.9 1.2 fusion.101
  256.0 1.2 fusion.99
  261.0 1.2 fusion.99
  266.1 1.2 fusion.99
  269.1 1.2 fusion.101
  271.1 1.2 fusion.99
  276.2 1.2 fusion.99
  281.3 1.2 fusion.99
  286.3 1.2 fusion.99
  291.4 1.2 fusion.99
  296.5 1.2 fusion.99
  301.5 1.2 fusion.99
  305.8 1.3 copy-done.1
  307.2 216.1 %reduce-scatter.2.cloned.1.call-done = bf16[128,256]{1,0:T(8,128)(2,1)} async-done(((bf16[4096,256]{1,0:T(8,128)(2,1)}), bf16[128,256]{1,0:T(8,128)(2,1)}) %reduce-scatter.2.cloned.1.call-update) | async-done | bytes 65552 | tf_op jit(solution)/shard_map/reduce_scatter | solution.py:146
  523.3 1.5 multiply_convert_fusion
  524.8 10.3 %all-to-all-start.2 = ((bf16[8,16,128]{2,1,0:T(8,128)(2,1)}), bf16[8,16,128]{2,1,0:T(8,128)(2,1)S(1)}, u32[]{:S(2)}, u32[]{:S(2)}) async-start(bf16[8,16,128]{2,1,0:T(8,128)(2,1)} %bitcast.14), calls=%async_computation.3 | async-start | bytes 65536 | tf_op jit(solution)/shard_map/all_to_all | solution.py:155
  537.6 2.2 all-to-all-done.2
  539.8 4.0 all-to-all-start.3
  544.4 4.1 all-to-all-done.3
  (387 shorter events, 99.7 us)
Async XLA Ops:
  7.2 0.8 copy-start
  7.2 24.5 %copy-start.4 = (s32[32]{0:T(128)S(1)}, s32[32]{0:T(128)}, u32[]{:S(2)}) copy-start(s32[32]{0:T(128)} %param.15) | copy-start | bytes 388
  7.2 83.8 %all-gather.3.cloned.1.call-start = ((), (), s32[]{:S(2)}) async-start(), calls=%async_computation.5 | async-start | bytes 1081344 | tf_op jit(solution)/shard_map/all_gather | solution.py:92
  18.9 148.6 %all-gather.5.cloned.1.call-start = ((), (), s32[]{:S(2)}) async-start(), calls=%async_computation.6 | async-start | bytes 1081344 | tf_op jit(solution)/shard_map/all_gather | solution.py:93
  28.2 495.1 %reduce-scatter.2.cloned.1.call-start = ((), (), s32[]{:S(2)}) async-start(), calls=%async_computation.7 | async-start | bytes 2162688 | tf_op jit(solution)/shard_map/reduce_scatter | solution.py:146
  305.8 1.3 copy-start.1
  305.8 229.3 %copy-start.2 = (bf16[1,8,128,128]{2,3,1,0:T(8,128)(2,1)S(1)}, bf16[1,8,128,128]{2,3,1,0:T(8,128)(2,1)}, u32[]{:S(2)}) copy-start(bf16[1,8,128,128]{2,3,1,0:T(8,128)(2,1)} %get-tuple-element.949) | copy-start | bytes 786436
  523.3 13.6 %copy-start.3 = (bf16[128,256]{1,0:T(8,128)(2,1)S(1)}, bf16[128,256]{1,0:T(8,128)(2,1)}, u32[]{:S(2)}) copy-start(bf16[128,256]{1,0:T(8,128)(2,1)} %reduce-scatter.2.cloned.1.call-done) | copy-start | bytes 196612
  524.8 15.0 %all-to-all-start.2 = ((bf16[8,16,128]{2,1,0:T(8,128)(2,1)}), bf16[8,16,128]{2,1,0:T(8,128)(2,1)S(1)}, u32[]{:S(2)}, u32[]{:S(2)}) async-start(bf16[8,16,128]{2,1,0:T(8,128)(2,1)} %bitcast.14), calls=%async_computation.3 | async-start | bytes 65536 | tf_op jit(solution)/shard_map/all_to_all | solution.py:155
  539.8 8.7 %all-to-all-start.3 = ((bf16[8,16,128]{2,1,0:T(8,128)(2,1)}), bf16[8,16,128]{2,1,0:T(8,128)(2,1)S(1)}, u32[]{:S(2)}, u32[]{:S(2)}) async-start(bf16[8,16,128]{2,1,0:T(8,128)(2,1)} %bitcast.16), calls=%async_computation.4 | async-start | bytes 65536 | tf_op jit(solution)/shard_map/all_to_all | solution.py:158
Sparse Core Ops, SparseCore 0:
  19.0 71.9 all-gather.2
  93.6 73.8 all-gather.4
  307.3 215.9 reduce-scatter.1
where the time goes:
time: 560 us; the launch traced here: 556 us
  waiting for transfers between devices  358 us (64%)
  matrix products  106 us (19%)
  other arithmetic  25.9 us (5%)
  blocking collectives  19.4 us (3%)
  local copies, waits for them, and re-layouts  14.7 us (3%)
  starting transfers between devices  14.4 us (3%)
  between operations  13.9 us (2%)
    reduce_scatter x1, waiting for transfers between devices, per_device(): lax.psum_scatter(buffer.astype(jnp.bfloat16), 'leaf', scatter_dimension=0...  216 us
    all_gather x1, waiting for transfers between devices, per_device(): value_piece = lax.all_gather(value_local, 'leaf', axis=0, tiled=True)  76.5 us
    all_gather x1, waiting for transfers between devices, per_device(): key_piece = lax.all_gather(key_local, 'leaf', axis=0, tiled=True)  59.2 us
    dot_general x32, matrix products, logits_of(): jnp.einsum('tkgd,skd->kgts', query_group, key_rows, preferred_element_typ...  37.6 us
    dot_general x16, matrix products, forward_tile(): jnp.einsum('kgts,skd->kgtd', expo.astype(jnp.bfloat16), value_rows, prefe...  21.8 us
    dot_general x16, matrix products, update_both(): jnp.einsum('kgts,skd->tkgd', dlogit, key_rows, preferred_element_type=jnp...  18.5 us
    dot_general x16, matrix products, gradient_tile(): jnp.einsum('tkgd,skd->kgts', grad_group, value_rows, preferred_element_ty...  18.1 us
    reduce_or x32, other arithmetic, visible(): jnp.any(ancestor_rows[:, :, None] == key_tag[None, None, :], axis=1)  13 us
  transfers between devices with their start and end apart: 5, of which 5 were waited for; matrix products, arithmetic and copies ran while one was open for 1% of the time, Pallas kernels for 0%

commit v1 on v0

--- a/solution.py
+++ b/solution.py
@@ -90,7 +90,9 @@
         jnp.zeros((key_heads, group, rows, HD), jnp.float32),
     )
     key_piece = lax.all_gather(key_local, "leaf", axis=0, tiled=True)
-    value_piece = lax.all_gather(value_local, "leaf", axis=0, tiled=True)
+    value_piece = jnp.concatenate(
+        lax.all_to_all(jnp.stack([value_local] * lax.axis_size("leaf")), "leaf", 0, 0), axis=0
+    )
 
     def update(inner, offset, tile_width):
         key_tile = lax.dynamic_slice_in_dim(key_piece, offset, tile_width, 0)

time: 560 us -> 514 us (0.918)
  waiting for transfers between devices: 358 us -> 325 us
  starting transfers between devices: 14.4 us -> 35.3 us
  blocking collectives: 19.4 us -> 0 us
  matrix products: 106 us -> 92.5 us
    all_gather x1, waiting for transfers between devices: 76.5 us -> 33.3 us  [per_device(): lax.all_gather(value_local, 'leaf', axis=0, tiled=True)]
    all_to_all x0 -> x3, starting transfers between devices: none -> 21 us  [the longest x1 10.5 us: per_device(): lax.all_to_all(jnp.stack([value_local] * lax.axis_size('leaf')), 'leaf',...]
    all_to_all x2 -> x0, blocking collectives: 19.4 us -> none  [the longest x1 11 us: per_device(): lax.all_to_all(key_in, 'head', split_axis=1, concat_axis=0, tiled=True)]
    dot_general x16, matrix products: 21.8 us -> 8.41 us  [forward_tile(): jnp.einsum('kgts,skd->kgtd', expo.astype(jnp.bfloat16), value_rows, prefe...]
    all_to_all x0 -> x3, waiting for transfers between devices: none -> 7.38 us  [the longest x1 4.02 us: per_device(): lax.all_to_all(value_in, 'head', split_axis=1, concat_axis=0, tiled=True)]
  transfers between devices with their start and end apart: 5 -> 8, of which waited for: 5 -> 7; matrix products, arithmetic and copies ran while one was open for 1% -> 10% of each run, Pallas kernels for 0% -> 0%
where the time goes in v1:
time: 514 us; the launch traced here: 510 us
  waiting for transfers between devices  325 us (63%)
  matrix products  92.5 us (18%)
  starting transfers between devices  35.3 us (7%)
  other arithmetic  25.9 us (5%)
  local copies, waits for them, and re-layouts  14.7 us (3%)
  between operations  14 us (3%)
    reduce_scatter x1, waiting for transfers between devices, per_device(): lax.psum_scatter(buffer.astype(jnp.bfloat16), 'leaf', scatter_dimension=0...  216 us
    all_gather x1, waiting for transfers between devices, per_device(): key_piece = lax.all_gather(key_local, 'leaf', axis=0, tiled=True)  61.1 us
    dot_general x32, matrix products, logits_of(): jnp.einsum('tkgd,skd->kgts', query_group, key_rows, preferred_element_typ...  37.6 us
    all_gather x1, waiting for transfers between devices, per_device(): lax.all_gather(value_local, 'leaf', axis=0, tiled=True)  33.3 us
    dot_general x16, matrix products, update_both(): jnp.einsum('kgts,skd->tkgd', dlogit, key_rows, preferred_element_type=jnp...  18.5 us
    dot_general x16, matrix products, gradient_tile(): jnp.einsum('tkgd,skd->kgts', grad_group, value_rows, preferred_element_ty...  18.1 us
    reduce_or x32, other arithmetic, visible(): jnp.any(ancestor_rows[:, :, None] == key_tag[None, None, :], axis=1)  13 us
    all_to_all x1, starting transfers between devices, per_device(): lax.all_to_all(jnp.stack([value_local] * lax.axis_size('leaf')), 'leaf',...  10.5 us
  transfers between devices with their start and end apart: 8, of which 7 were waited for; matrix products, arithmetic and copies ran while one was open for 10% of the time, Pallas kernels for 0%

profile of v1, /device:TPU:1, one launch (start us, length us, event | category | flops | bytes accessed | tf_op | source)
XLA Modules:
  0.0 510.5 jit_solution(13447978047050331390)
XLA Ops:
  8.6 6.4 %all-to-all-start = ((bf16[16,8,128]{2,0,1:T(8,128)(2,1)}), bf16[16,8,128]{2,0,1:T(8,128)(2,1)S(1)}, u32[]{:S(2)}, u32[]{:S(2)}) async-start(bf16[16,8,128]{2,0,1:T(8,128)(2,1)} %copy_bitcast_fusion.3), calls=%async_computation | async-start | bytes 65536 | tf_op jit(solution)/shard_map/all_to_all | solution.py:73
  15.0 1.4 copy_bitcast_fusion.2
  16.4 3.4 all-to-all-done
  19.7 4.0 all-to-all-start.1
  24.4 4.0 all-to-all-done.1
  28.5 1.2 stack.5
  29.7 10.5 %all-to-all-start.2 = ((bf16[32,128,128]{2,1,0:T(8,128)(2,1)}), bf16[32,128,128]{2,1,0:T(8,128)(2,1)S(1)}, u32[]{:S(2)}, u32[]{:S(2)}) async-start(bf16[32,128,128]{2,1,0:T(8,128)(2,1)} %stack.5), calls=%async_computation.2 | async-start | bytes 2097152 | tf_op jit(solution)/shard_map/all_to_all | solution.py:94
  41.3 61.1 %all-gather.3.cloned.1.call-done = bf16[4096,128]{1,0:T(8,128)(2,1)} async-done(((bf16[128,128]{1,0:T(8,128)(2,1)}), bf16[4096,128]{1,0:T(8,128)(2,1)}) %all-gather.3.cloned.1.call-update) | async-done | bytes 1048592 | tf_op jit(solution)/shard_map/all_gather | solution.py:92
  102.4 42.8 %while.44 = (s32[]{:T(128)}, f32[1,8,128]{2,1,0:T(8,128)S(1)}, f32[1,8,128]{2,1,0:T(8,128)S(1)}, f32[1,8,128,128]{3,2,1,0:T(8,128)S(1)}, s32[128,8]{1,0:T(8,128)...) while((s32[]{:T(128)}, f32[1,8,128]{2,1,0:T(8,128)S(1)}, ...), condition=%wide.region_4.5_spmd.clone.clone.clone, body=%wide.region_0.4_spmd.clone.clone.clone.sunk | while | flops 137082496 | bytes 4862171 | solution.py:17
  146.2 33.3 %all-gather.5.cloned.1.call-done = bf16[4096,128]{1,0:T(8,128)(2,1)} async-done(((bf16[128,128]{1,0:T(8,128)(2,1)}), bf16[4096,128]{1,0:T(8,128)(2,1)}) %all-gather.5.cloned.1.call-update) | async-done | bytes 1048592 | tf_op jit(solution)/shard_map/all_gather | solution.py:107
  179.7 81.0 %while.45 = (s32[]{:T(128)}, f32[128,1,8,128]{0,3,2,1:T(8,128)S(1)}, bf16[4096,256]{1,0:T(8,128)(2,1)S(1)}, bf16[4096,128]{1,0:T(8,128)(2,1)}, s32[128,8]{1,0:T(...) while((s32[]{:T(128)}, ...), condition=%wide.region_8.9_spmd.clone.clone.clone, body=%wide.region_6.8_spmd.clone.clone.clone.sunk | while | flops 338534016 | bytes 8147185 | solution.py:17
  180.4 1.2 fusion.99
  185.5 1.2 fusion.99
  188.5 1.2 fusion.101
  190.5 1.2 fusion.99
  193.5 1.2 fusion.101
  195.6 1.2 fusion.99
  198.6 1.2 fusion.101
  200.7 1.2 fusion.99
  203.6 1.2 fusion.101
  205.7 1.2 fusion.99
  208.7 1.2 fusion.101
  210.8 1.2 fusion.99
  213.8 1.2 fusion.101
  215.8 1.2 fusion.99
  218.8 1.2 fusion.101
  220.9 1.2 fusion.99
  223.9 1.2 fusion.101
  226.0 1.2 fusion.99
  228.9 1.2 fusion.101
  231.0 1.2 fusion.99
  234.0 1.2 fusion.101
  236.1 1.2 fusion.99
  239.1 1.2 fusion.101
  241.2 1.2 fusion.99
  244.1 1.2 fusion.101
  246.2 1.2 fusion.99
  249.2 1.2 fusion.101
  251.3 1.2 fusion.99
  256.3 1.2 fusion.99
  259.3 1.2 fusion.101
  260.7 1.3 copy-done.1
  262.0 216.1 %reduce-scatter.2.cloned.1.call-done = bf16[128,256]{1,0:T(8,128)(2,1)} async-done(((bf16[4096,256]{1,0:T(8,128)(2,1)}), bf16[128,256]{1,0:T(8,128)(2,1)}) %reduce-scatter.2.cloned.1.call-update) | async-done | bytes 65552 | tf_op jit(solution)/shard_map/reduce_scatter | solution.py:148
  478.1 1.5 multiply_convert_fusion
  479.6 10.3 %all-to-all-start.3 = ((bf16[8,16,128]{2,1,0:T(8,128)(2,1)}), bf16[8,16,128]{2,1,0:T(8,128)(2,1)S(1)}, u32[]{:S(2)}, u32[]{:S(2)}) async-start(bf16[8,16,128]{2,1,0:T(8,128)(2,1)} %bitcast.16), calls=%async_computation.4 | async-start | bytes 65536 | tf_op jit(solution)/shard_map/all_to_all | solution.py:157
  492.4 2.2 all-to-all-done.3
  494.6 4.0 all-to-all-start.4
  499.2 4.1 all-to-all-done.4
  (402 shorter events, 93.3 us)
Async XLA Ops:
  7.2 0.8 copy-start
  7.2 33.1 %copy-start.8 = (s32[32,8]{0,1:T(8,128)S(1)}, s32[32,8]{0,1:T(8,128)}, u32[]{:S(2)}) copy-start(s32[32,8]{0,1:T(8,128)} %param.14) | copy-start | bytes 3076
  7.2 33.2 %copy-start.4 = (bf16[128,1024]{1,0:T(8,128)(2,1)S(1)}, bf16[128,1024]{1,0:T(8,128)(2,1)}, u32[]{:S(2)}) copy-start(bf16[128,1024]{1,0:T(8,128)(2,1)} %param.10) | copy-start | bytes 786436
  8.6 11.2 %all-to-all-start = ((bf16[16,8,128]{2,0,1:T(8,128)(2,1)}), bf16[16,8,128]{2,0,1:T(8,128)(2,1)S(1)}, u32[]{:S(2)}, u32[]{:S(2)}) async-start(bf16[16,8,128]{2,0,1:T(8,128)(2,1)} %copy_bitcast_fusion.3), calls=%async_computation | async-start | bytes 65536 | tf_op jit(solution)/shard_map/all_to_all | solution.py:73
  19.7 4.0 copy-start.6
  19.7 8.7 %all-to-all-start.1 = ((bf16[16,8,128]{2,0,1:T(8,128)(2,1)}), bf16[16,8,128]{2,0,1:T(8,128)(2,1)S(1)}, u32[]{:S(2)}, u32[]{:S(2)}) async-start(bf16[16,8,128]{2,0,1:T(8,128)(2,1)} %copy_bitcast_fusion.2), calls=%async_computation.1 | async-start | bytes 65536 | tf_op jit(solution)/shard_map/all_to_all | solution.py:74
  23.7 78.7 %all-gather.3.cloned.1.call-start = ((), (), s32[]{:S(2)}) async-start(), calls=%async_computation.6 | async-start | bytes 1081344 | tf_op jit(solution)/shard_map/all_gather | solution.py:92
  28.5 12.3 %copy-start.3 = (bf16[16,8,128]{2,0,1:T(8,128)(2,1)}, bf16[16,8,128]{2,0,1:T(8,128)(2,1)S(1)}, u32[]{:S(2)}) copy-start(bf16[16,8,128]{2,0,1:T(8,128)(2,1)S(1)} %all-to-all-done.1) | copy-start | bytes 98308
  28.5 12.3 %copy-start.5 = (bf16[128,1024]{1,0:T(8,128)(2,1)S(1)}, bf16[128,1024]{1,0:T(8,128)(2,1)}, u32[]{:S(2)}) copy-start(bf16[128,1024]{1,0:T(8,128)(2,1)} %param.13) | copy-start | bytes 786436
  29.7 72.7 %all-to-all-start.2 = ((bf16[32,128,128]{2,1,0:T(8,128)(2,1)}), bf16[32,128,128]{2,1,0:T(8,128)(2,1)S(1)}, u32[]{:S(2)}, u32[]{:S(2)}) async-start(bf16[32,128,128]{2,1,0:T(8,128)(2,1)} %stack.5), calls=%async_computation.2 | async-start | bytes 2097152 | tf_op jit(solution)/shard_map/all_to_all | solution.py:94
  40.2 0.9 copy-start.9
  40.2 139.3 %all-gather.5.cloned.1.call-start = ((), (), s32[]{:S(2)}) async-start(), calls=%async_computation.7 | async-start | bytes 1081344 | tf_op jit(solution)/shard_map/all_gather | solution.py:107
  41.2 436.9 %reduce-scatter.2.cloned.1.call-start = ((), (), s32[]{:S(2)}) async-start(), calls=%async_computation.8 | async-start | bytes 2162688 | tf_op jit(solution)/shard_map/reduce_scatter | solution.py:148
  260.6 1.3 copy-start.1
  260.6 229.3 %copy-start.2 = (bf16[1,8,128,128]{2,3,1,0:T(8,128)(2,1)S(1)}, bf16[1,8,128,128]{2,3,1,0:T(8,128)(2,1)}, u32[]{:S(2)}) copy-start(bf16[1,8,128,128]{2,3,1,0:T(8,128)(2,1)} %get-tuple-element.949) | copy-start | bytes 786436
  478.1 13.6 %copy-start.7 = (bf16[128,256]{1,0:T(8,128)(2,1)S(1)}, bf16[128,256]{1,0:T(8,128)(2,1)}, u32[]{:S(2)}) copy-start(bf16[128,256]{1,0:T(8,128)(2,1)} %reduce-scatter.2.cloned.1.call-done) | copy-start | bytes 196612
  479.6 15.0 %all-to-all-start.3 = ((bf16[8,16,128]{2,1,0:T(8,128)(2,1)}), bf16[8,16,128]{2,1,0:T(8,128)(2,1)S(1)}, u32[]{:S(2)}, u32[]{:S(2)}) async-start(bf16[8,16,128]{2,1,0:T(8,128)(2,1)} %bitcast.16), calls=%async_computation.4 | async-start | bytes 65536 | tf_op jit(solution)/shard_map/all_to_all | solution.py:157
  494.6 8.7 %all-to-all-start.4 = ((bf16[8,16,128]{2,1,0:T(8,128)(2,1)}), bf16[8,16,128]{2,1,0:T(8,128)(2,1)S(1)}, u32[]{:S(2)}, u32[]{:S(2)}) async-start(bf16[8,16,128]{2,1,0:T(8,128)(2,1)} %bitcast.18), calls=%async_computation.5 | async-start | bytes 65536 | tf_op jit(solution)/shard_map/all_to_all | solution.py:160
Sparse Core Ops, SparseCore 0:
  27.7 74.6 all-gather.2
  105.6 73.9 all-gather.4
  262.1 215.9 reduce-scatter.1
